TPU v7x, 32 devices: a whole 2x2x4 slice. The times are simulated.
32 devices in a mesh: grp: 2 (over x), samp: 16 (over z, y, core).
Axes of the slice: x: 2, y: 2, z: 4, core: 2. Of those that a mesh axis runs over, the one named last changes fastest.
Arguments:
- genotypes: int32 [32768, 2048], P(('grp', 'samp')), parts along dimension 0, may hold values from 0 to 2
- probe_signs: int32 [32, 32768], P(None, ('grp', 'samp')), parts along dimension 1, may hold values from 0 to 1
- phenotype: float32 [32768], P(('grp', 'samp')), parts along dimension 0, may hold values from -6 to 6
- marker_mean: float32 [2048], replicated, may hold values from 0.2 to 1.8
- marker_scale: float32 [2048], replicated, may hold values from 0.5 to 4
- marker_bin: int32 [2048], replicated, may hold values from 0 to 15, as said below
Outputs:
- products: float32 [16, 33, 32768], P(None, None, ('grp', 'samp')), parts along dimension 2
- gram: float32 [32, 16, 33], P('grp'), parts along dimension 0
There are 2 independent parts, one for each index of `grp`. A program takes and returns all parts, laid end to end along the dimension named above; an argument that names none is the same for every part. Nothing has to cross between parts.
Inputs may be any that keep to these rules, and one draw needn't show every extreme that they name: `marker_bin`: every bin holds exactly 128 markers.
All inputs are finite; a program needn't handle non-finite values.
Results may differ from a plain program's by a relative error of at most 0.0001.
Values sent between devices are 32-bit elements; how exact they have to be, the bound alone decides.
A program may use at most 128 MiB of HBM per device.

v0:
```python
import jax
import jax.numpy as jnp
from jax import lax
from jax.sharding import PartitionSpec as P

BINS = 16
M_BIN = 128


def shards(genotypes, probe_signs, phenotype, marker_mean, marker_scale, marker_bin):
    samples = genotypes.shape[0]
    devices = lax.axis_size("samp")
    total = jnp.float32(samples * devices)
    order = jnp.argsort(marker_bin, stable=True)
    picked = jnp.take(genotypes, order, axis=1).astype(jnp.float32)
    standard = (picked - marker_mean[order]) * marker_scale[order]
    vectors = jnp.concatenate(
        [(2 * probe_signs - 1).astype(jnp.float32), phenotype[None, :]], axis=0
    )
    share = lax.psum_scatter(
        jnp.dot(
            standard.T,
            vectors.T,
            precision=lax.Precision.HIGHEST,
            preferred_element_type=jnp.float32,
        ),
        "samp",
        scatter_dimension=0,
        tiled=True,
    )
    scores = lax.all_gather(share, "samp", axis=0, tiled=True)
    scores = scores / jnp.sqrt(total)
    blocks = standard.reshape(samples, BINS, M_BIN)
    weights = scores.reshape(BINS, M_BIN, scores.shape[1])
    products = jnp.einsum(
        "skm,kmr->krs", blocks, weights, precision=lax.Precision.HIGHEST
    ) / jnp.sqrt(jnp.float32(M_BIN))
    local_gram = jnp.einsum("krs,lrs->klr", products, products, precision=lax.Precision.HIGHEST)
    gram = lax.psum(local_gram, "samp") / total
    return (products, gram)


def solution(mesh):
    in_specs = (
        P(("grp", "samp"), None),
        P(None, ("grp", "samp")),
        P(("grp", "samp")),
        P(),
        P(),
        P(),
    )
    out_specs = (P(None, None, ("grp", "samp")), P("grp", None, None))
    return jax.shard_map(shards, mesh=mesh, in_specs=in_specs, out_specs=out_specs, check_vma=False)
```

profile of v0, /device:TPU:0, one launch (start us, length us, event | category | flops | bytes accessed | tf_op | source)
XLA Modules:
  0.0 233.8 jit_solution(9177498620670587703)
XLA Ops:
  7.2 0.0 copy-start
  7.2 0.0 copy-start.1
  7.2 0.0 reduce-scatter.2.cloned.1.call-start
  7.2 5.7 %sort.17 = (s32[2048]{0:T(1024)}, s32[2048]{0:T(1024)S(1)}) sort(s32[2048]{0:T(1024)} %param.11, s32[2048]{0:T(1024)S(1)} %iota.4), dimensions={0}, to_apply=%region_0.0 | sort | flops 22528 | bytes 32768 | tf_op jit(solution)/shard_map/jit(argsort)/sort | solution.py:14
  13.0 0.0 copy-done
  13.0 0.0 copy-start.3
  13.0 11.8 %gather_fusion.2 = f32[2048]{0:T(1024)S(1)} fusion(f32[2048]{0:T(1024)S(1)} %copy-done, s32[2048]{0:T(1024)S(1)} %fusion.25), kind=kCustom, calls=%fused_computation.2 | custom fusion | bytes 24576 | tf_op jit(solution)/shard_map/gather | solution.py:16
  24.8 0.0 copy-done.1
  24.8 11.8 %gather_fusion.1 = f32[2048]{0:T(1024)S(1)} fusion(f32[2048]{0:T(1024)S(1)} %copy-done.1, s32[2048]{0:T(1024)S(1)} %fusion.25), kind=kCustom, calls=%fused_computation.1 | custom fusion | bytes 24576 | tf_op jit(solution)/shard_map/gather | solution.py:16
  36.6 0.0 copy-done.3
  36.6 9.3 %copy.15 = s32[1024,2048]{0,1:T(8,128)} copy(s32[1024,2048]{1,0:T(8,128)} %param.6) | data formatting | bytes 16777216 | tf_op args[0]
  45.9 0.0 copy-start.4
  45.9 15.1 %gather_fusion = s32[2048,1024]{1,0:T(8,128)} fusion(s32[1024,2048]{0,1:T(8,128)} %copy.15, s32[2048]{0:T(1024)S(1)} %fusion.25), kind=kCustom, calls=%fused_computation | custom fusion | bytes 16785408 | tf_op jit(solution)/shard_map/jit(_take)/gather | solution.py:15
  61.1 0.0 copy-done.4
  61.1 12.3 %fusion.3 = f32[2048,33]{0,1:T(8,128)} fusion(s32[2048,1024]{1,0:T(8,128)} %gather_fusion, f32[2048]{0:T(1024)S(1)} %gather_fusion.2, f32[2048]{0:T(1024)S(1)} %gather_fusion.1, pred[2048]{0:T(1024)(128)(4,1)S(1)} %compare_and_fusion, f32[1,1024]{1,0:T(1,128)S(1)} %bitcast.31, f32[32,1024]{1,0:T(8,128)S(1)} %add_convert_fusion), kind=kOutput, calls=%fused_computation.7 | convolution fusion | flops 838894592 | bytes 8812544 | tf_op jit(solution)/shard_map/dot_general | solution.py:21
  73.3 0.0 reduce-scatter.2.cloned.1.call-update
  73.4 9.3 %copy.16 = s32[1024,16,128]{2,0,1:T(8,128)} copy(s32[1024,16,128]{0,2,1:T(8,128)} %bitcast.26) | data formatting | bytes 16777216 | tf_op jit(solution)/shard_map/jit(_take)/gather | solution.py:15
  82.6 45.9 %reduce-scatter.2.cloned.1.call-done = f32[128,33]{0,1:T(8,128)} async-done(((f32[2048,33]{0,1:T(8,128)}), f32[128,33]{0,1:T(8,128)}) %reduce-scatter.2.cloned.1.call-update) | async-done | bytes 16912 | tf_op jit(solution)/shard_map/reduce_scatter | solution.py:20
  128.6 20.7 %all_gather.3 = f32[2048,33]{0,1:T(8,128)S(1)} all-gather(f32[128,33]{0,1:T(8,128)} %reduce-scatter.2.cloned.1.call-done), channel_id=1, replica_groups=mesh['grp'=2,'samp'=16] {'samp'}, dimensions={0}, use_global_device_ids=true | all-gather | bytes 287232 | tf_op jit(solution)/shard_map/all_gather | solution.py:31
  149.3 0.1 copy.22
  149.4 11.3 %fusion.18 = f32[16,33,1024]{2,1,0:T(8,128)S(1)} fusion(s32[1024,16,128]{2,0,1:T(8,128)} %copy.16, f32[16,128]{1,0:T(8,128)S(1)} %bitcast.29, f32[16,128]{1,0:T(8,128)S(1)} %bitcast.30, pred[16,128]{1,0:T(8,128)(4,1)S(1)} %fusion.31, f32[16,128,33]{1,0,2:T(8,128)S(1)} %slice_bitcast_fusion), kind=kOutput, calls=%fused_computation.21 | convolution fusion | flops 839401472 | bytes 10840064 | tf_op jit(solution)/shard_map/skm,kmr->krs/dot_general | solution.py:35
  160.7 1.3 copy.20
  161.9 0.0 copy-start.2
  162.0 3.1 %convolution_bitcast_fusion = f32[16,16,33]{0,1,2:T(8,128)S(1)} fusion(f32[16,33,1024]{2,0,1:T(8,128)S(1)} %copy.20), kind=kOutput, calls=%fused_computation.22 | convolution fusion | flops 103809024 | bytes 2196480 | tf_op jit(solution)/shard_map/krs,lrs->klr/dot_general | solution.py:38
  165.1 61.0 %psum.7 = f32[16,16,33]{0,1,2:T(8,128)S(1)} all-reduce(f32[16,16,33]{0,1,2:T(8,128)S(1)} %convolution_bitcast_fusion), channel_id=1, replica_groups=mesh['grp'=2,'samp'=16] {'samp'}, use_global_device_ids=true, to_apply=%region_2.3 | all-reduce | flops 8448 | bytes 67584 | tf_op jit(solution)/shard_map/psum | solution.py:39
  226.1 0.8 copy.21
  227.0 0.0 copy-done.2
  (8 shorter events, 0.1 us)
Async XLA Ops:
  7.2 5.8 %copy-start = (f32[2048]{0:T(1024)S(1)}, f32[2048]{0:T(1024)}, u32[]{:S(2)}) copy-start(f32[2048]{0:T(1024)} %param.10) | copy-start | bytes 24580
  7.2 17.6 %copy-start.1 = (f32[2048]{0:T(1024)S(1)}, f32[2048]{0:T(1024)}, u32[]{:S(2)}) copy-start(f32[2048]{0:T(1024)} %param.9) | copy-start | bytes 24580
  7.2 121.4 %reduce-scatter.2.cloned.1.call-start = ((), (), s32[]{:S(2)}) async-start(), calls=%async_computation.1 | async-start | bytes 348160 | tf_op jit(solution)/shard_map/reduce_scatter | solution.py:20
  13.0 23.6 %copy-start.3 = (s32[32,1024]{1,0:T(8,128)S(1)}, s32[32,1024]{1,0:T(8,128)}, u32[]{:S(2)}) copy-start(s32[32,1024]{1,0:T(8,128)} %param.7) | copy-start | bytes 393220
  45.9 15.2 %copy-start.4 = (f32[1024]{0:T(1024)S(1)}, f32[1024]{0:T(1024)}, u32[]{:S(2)}) copy-start(f32[1024]{0:T(1024)} %param.8) | copy-start | bytes 12292
  161.9 65.0 %copy-start.2 = (f32[16,33,1024]{2,0,1:T(8,128)}, f32[16,33,1024]{2,0,1:T(8,128)S(1)}, u32[]{:S(2)}) copy-start(f32[16,33,1024]{2,0,1:T(8,128)S(1)} %copy.20) | copy-start | bytes 6488068
Sparse Core Ops, SparseCore 0:
  73.5 55.0 reduce-scatter.1
where the time goes:
time: 234 us
  blocking collectives  81.7 us (35%)
  local copies, waits for them, and re-layouts  59.5 us (25%)
  waiting for transfers between devices  45.9 us (20%)
  matrix products  26.7 us (11%)
  between operations  14.2 us (6%)
  other arithmetic  5.82 us (2%)
    psum x1, blocking collectives, shards(): gram = lax.psum(local_gram, 'samp') / total  61 us
    reduce_scatter x1, waiting for transfers between devices, shards(): lax.psum_scatter(jnp.dot(standard.T, vectors.T, precision=lax.Precision.H...  45.9 us
    gather x2, local copies, waits for them, and re-layouts, shards(): picked = jnp.take(genotypes, order, axis=1).astype(jnp.float32)  24.4 us
    gather x2, local copies, waits for them, and re-layouts, shards(): standard = (picked - marker_mean[order]) * marker_scale[order]  23.6 us
    all_gather x1, blocking collectives, shards(): scores = lax.all_gather(share, 'samp', axis=0, tiled=True)  20.7 us
    dot_general x1, matrix products, shards(): jnp.dot(standard.T, vectors.T, precision=lax.Precision.HIGHEST, preferred...  12.3 us
    unnamed x14, local copies, waits for them, and re-layouts  11.5 us
    dot_general x1, matrix products, shards(): jnp.einsum('skm,kmr->krs', blocks, weights, precision=lax.Precision.HIGHEST)  11.3 us
  transfers between devices with their start and end apart: 1, of which 1 were waited for; matrix products, arithmetic and copies ran while one was open for 4% of the time, Pallas kernels for 0%

commit v1 on v0

--- a/solution.py
+++ b/solution.py
@@ -36,7 +36,7 @@
         "skm,kmr->krs", blocks, weights, precision=lax.Precision.HIGHEST
     ) / jnp.sqrt(jnp.float32(M_BIN))
     local_gram = jnp.einsum("krs,lrs->klr", products, products, precision=lax.Precision.HIGHEST)
-    gram = lax.psum(local_gram, "samp") / total
+    gram = jnp.sum(lax.all_gather(local_gram, "samp"), axis=0) / total
     return (products, gram)
 
 

time: 234 us -> 205 us (0.88)
  blocking collectives: 81.7 us -> 50.3 us
  other arithmetic: 5.82 us -> 8.21 us
    psum x1 -> x0, blocking collectives: 61 us -> none  [shards(): gram = lax.psum(local_gram, 'samp') / total]
    all_gather x0 -> x1, blocking collectives: none -> 29.5 us  [shards(): gram = jnp.sum(lax.all_gather(local_gram, 'samp'), axis=0) / total]
    unnamed x14 -> x13, local copies, waits for them, and re-layouts: 11.5 us -> 10.6 us
  transfers between devices with their start and end apart: 1 -> 1, of which waited for: 1 -> 1; matrix products, arithmetic and copies ran while one was open for 4% -> 5% of each run, Pallas kernels for 0% -> 0%
where the time goes in v1:
time: 205 us; the launch traced here: 204 us
  local copies, waits for them, and re-layouts  58.8 us (29%)
  blocking collectives  50.3 us (25%)
  waiting for transfers between devices  45.9 us (22%)
  matrix products  26.7 us (13%)
  between operations  14.2 us (7%)
  other arithmetic  8.21 us (4%)
    reduce_scatter x1, waiting for transfers between devices, shards(): lax.psum_scatter(jnp.dot(standard.T, vectors.T, precision=lax.Precision.H...  45.9 us
    all_gather x1, blocking collectives, shards(): gram = jnp.sum(lax.all_gather(local_gram, 'samp'), axis=0) / total  29.5 us
    gather x2, local copies, waits for them, and re-layouts, shards(): picked = jnp.take(genotypes, order, axis=1).astype(jnp.float32)  24.4 us
    gather x2, local copies, waits for them, and re-layouts, shards(): standard = (picked - marker_mean[order]) * marker_scale[order]  23.6 us
    all_gather x1, blocking collectives, shards(): scores = lax.all_gather(share, 'samp', axis=0, tiled=True)  20.7 us
    dot_general x1, matrix products, shards(): jnp.dot(standard.T, vectors.T, precision=lax.Precision.HIGHEST, preferred...  12.3 us
    dot_general x1, matrix products, shards(): jnp.einsum('skm,kmr->krs', blocks, weights, precision=lax.Precision.HIGHEST)  11.3 us
    unnamed x13, local copies, waits for them, and re-layouts  10.6 us
  transfers between devices with their start and end apart: 1, of which 1 were waited for; matrix products, arithmetic and copies ran while one was open for 5% of the time, Pallas kernels for 0%

profile of v1, /device:TPU:0, one launch (start us, length us, event | category | flops | bytes accessed | tf_op | source)
XLA Modules:
  0.0 204.1 jit_solution(6415326989422621162)
XLA Ops:
  7.2 0.0 copy-start
  7.2 0.0 copy-start.1
  7.2 0.0 reduce-scatter.2.cloned.1.call-start
  7.2 5.7 %sort.17 = (s32[2048]{0:T(1024)}, s32[2048]{0:T(1024)S(1)}) sort(s32[2048]{0:T(1024)} %param.11, s32[2048]{0:T(1024)S(1)} %iota.4), dimensions={0}, to_apply=%region_0.0 | sort | flops 22528 | bytes 32768 | tf_op jit(solution)/shard_map/jit(argsort)/sort | solution.py:14
  13.0 0.0 copy-done
  13.0 0.0 copy-start.3
  13.0 11.8 %gather_fusion.2 = f32[2048]{0:T(1024)S(1)} fusion(f32[2048]{0:T(1024)S(1)} %copy-done, s32[2048]{0:T(1024)S(1)} %fusion.25), kind=kCustom, calls=%fused_computation.2 | custom fusion | bytes 24576 | tf_op jit(solution)/shard_map/gather | solution.py:16
  24.8 0.0 copy-done.1
  24.8 11.8 %gather_fusion.1 = f32[2048]{0:T(1024)S(1)} fusion(f32[2048]{0:T(1024)S(1)} %copy-done.1, s32[2048]{0:T(1024)S(1)} %fusion.25), kind=kCustom, calls=%fused_computation.1 | custom fusion | bytes 24576 | tf_op jit(solution)/shard_map/gather | solution.py:16
  36.6 0.0 copy-done.3
  36.6 9.3 %copy.21 = s32[1024,2048]{0,1:T(8,128)} copy(s32[1024,2048]{1,0:T(8,128)} %param.6) | data formatting | bytes 16777216 | tf_op args[0]
  45.9 0.0 copy-start.4
  45.9 15.1 %gather_fusion = s32[2048,1024]{1,0:T(8,128)} fusion(s32[1024,2048]{0,1:T(8,128)} %copy.21, s32[2048]{0:T(1024)S(1)} %fusion.25), kind=kCustom, calls=%fused_computation | custom fusion | bytes 16785408 | tf_op jit(solution)/shard_map/jit(_take)/gather | solution.py:15
  61.1 0.0 copy-done.4
  61.1 12.3 %fusion.3 = f32[2048,33]{0,1:T(8,128)} fusion(s32[2048,1024]{1,0:T(8,128)} %gather_fusion, f32[2048]{0:T(1024)S(1)} %gather_fusion.2, f32[2048]{0:T(1024)S(1)} %gather_fusion.1, pred[2048]{0:T(1024)(128)(4,1)S(1)} %compare_and_fusion, f32[1,1024]{1,0:T(1,128)S(1)} %bitcast.33, f32[32,1024]{1,0:T(8,128)S(1)} %add_convert_fusion), kind=kOutput, calls=%fused_computation.7 | convolution fusion | flops 838894592 | bytes 8812544 | tf_op jit(solution)/shard_map/dot_general | solution.py:21
  73.3 0.0 reduce-scatter.2.cloned.1.call-update
  73.4 9.3 %copy.22 = s32[1024,16,128]{2,0,1:T(8,128)} copy(s32[1024,16,128]{0,2,1:T(8,128)} %bitcast.27) | data formatting | bytes 16777216 | tf_op jit(solution)/shard_map/jit(_take)/gather | solution.py:15
  82.6 45.9 %reduce-scatter.2.cloned.1.call-done = f32[128,33]{0,1:T(8,128)} async-done(((f32[2048,33]{0,1:T(8,128)}), f32[128,33]{0,1:T(8,128)}) %reduce-scatter.2.cloned.1.call-update) | async-done | bytes 16912 | tf_op jit(solution)/shard_map/reduce_scatter | solution.py:20
  128.6 20.7 %all_gather.9 = f32[2048,33]{0,1:T(8,128)S(1)} all-gather(f32[128,33]{0,1:T(8,128)} %reduce-scatter.2.cloned.1.call-done), channel_id=1, replica_groups=mesh['grp'=2,'samp'=16] {'samp'}, dimensions={0}, use_global_device_ids=true | all-gather | bytes 287232 | tf_op jit(solution)/shard_map/all_gather | solution.py:31
  149.3 0.1 copy.28
  149.4 11.3 %fusion.18 = f32[16,33,1024]{2,1,0:T(8,128)S(1)} fusion(s32[1024,16,128]{2,0,1:T(8,128)} %copy.22, f32[16,128]{1,0:T(8,128)S(1)} %bitcast.31, f32[16,128]{1,0:T(8,128)S(1)} %bitcast.32, pred[16,128]{1,0:T(8,128)(4,1)S(1)} %fusion.31, f32[16,128,33]{1,0,2:T(8,128)S(1)} %slice_bitcast_fusion), kind=kOutput, calls=%fused_computation.21 | convolution fusion | flops 839401472 | bytes 10840064 | tf_op jit(solution)/shard_map/skm,kmr->krs/dot_general | solution.py:35
  160.7 1.3 copy.27
  161.9 0.0 copy-start.2
  162.0 3.1 %convolution_bitcast_fusion = f32[16,16,33]{0,1,2:T(8,128)S(1)} fusion(f32[16,33,1024]{2,0,1:T(8,128)S(1)} %copy.27), kind=kOutput, calls=%fused_computation.22 | convolution fusion | flops 103809024 | bytes 2196480 | tf_op jit(solution)/shard_map/krs,lrs->klr/dot_general | solution.py:38
  165.1 0.2 copy.26
  165.3 29.5 %all-gather = f32[256,16,33]{2,1,0:T(8,128)} all-gather(f32[16,16,33]{2,1,0:T(8,128)S(1)} %copy.26), channel_id=2, replica_groups=mesh['grp'=2,'samp'=16] {'samp'}, dimensions={0}, use_global_device_ids=true | all-gather | bytes 574464 | tf_op jit(solution)/shard_map/all_gather | solution.py:39
  194.8 1.8 reduce_sum.9
  196.6 0.7 broadcast_multiply_fusion.1
  197.2 0.0 copy-done.2
  (7 shorter events, 0.1 us)
Async XLA Ops:
  7.2 5.8 %copy-start = (f32[2048]{0:T(1024)S(1)}, f32[2048]{0:T(1024)}, u32[]{:S(2)}) copy-start(f32[2048]{0:T(1024)} %param.10) | copy-start | bytes 24580
  7.2 17.6 %copy-start.1 = (f32[2048]{0:T(1024)S(1)}, f32[2048]{0:T(1024)}, u32[]{:S(2)}) copy-start(f32[2048]{0:T(1024)} %param.9) | copy-start | bytes 24580
  7.2 121.4 %reduce-scatter.2.cloned.1.call-start = ((), (), s32[]{:S(2)}) async-start(), calls=%async_computation.1 | async-start | bytes 348160 | tf_op jit(solution)/shard_map/reduce_scatter | solution.py:20
  13.0 23.6 %copy-start.3 = (s32[32,1024]{1,0:T(8,128)S(1)}, s32[32,1024]{1,0:T(8,128)}, u32[]{:S(2)}) copy-start(s32[32,1024]{1,0:T(8,128)} %param.7) | copy-start | bytes 393220
  45.9 15.2 %copy-start.4 = (f32[1024]{0:T(1024)S(1)}, f32[1024]{0:T(1024)}, u32[]{:S(2)}) copy-start(f32[1024]{0:T(1024)} %param.8) | copy-start | bytes 12292
  161.9 35.3 %copy-start.2 = (f32[16,33,1024]{2,0,1:T(8,128)}, f32[16,33,1024]{2,0,1:T(8,128)S(1)}, u32[]{:S(2)}) copy-start(f32[16,33,1024]{2,0,1:T(8,128)S(1)} %copy.27) | copy-start | bytes 6488068
Sparse Core Ops, SparseCore 0:
  73.5 55.0 reduce-scatter.1
